TPU v7x, 256 devices: a whole 4x4x8 slice. The times are simulated.
256 devices in a mesh: rows: 8 (over x, core), pts: 32 (over y, z).
Axes of the slice: x: 4, y: 4, z: 8, core: 2. Of those that a mesh axis runs over, the one named last changes fastest.
Arguments:
- features: bfloat16 [32768, 128], P('pts'), may hold values from -6 to 6
- targets: bfloat16 [32768, 256], P('pts'), may hold values from -6 to 6
- coefficients: float32 [32768, 256], P('pts'), may hold values from -6 to 6
- momentum: float32 [32768, 256], P('pts'), may hold values from -6 to 6
- block_index: int32 [2, 2048], replicated, may hold values from 0 to 32767, as said below
- pivot_index: int32 [2, 512], replicated, may hold values from 0 to 2047, as said below
- nystrom_core: bfloat16 [2, 512, 512], replicated, may hold values from -0.5 to 3
Outputs:
- new_coefficients: float32 [32768, 256], P('pts')
- new_momentum: float32 [32768, 256], P('pts')
Inputs may be any that keep to these rules, and one draw needn't show every extreme that they name: `block_index`: each row lists 2048 distinct points; a point p belongs to index p // 1024 of pts; in each row one index of pts, drawn from the seed, owns exactly 24 of the points in every aligned group of 256 positions, and no index owns more than 24 points of any such group. `pivot_index`: each row lists 512 distinct positions.
All inputs are finite; a program needn't handle non-finite values.
Results may differ from a plain program's by a relative error of at most 0.0041.
The roundings to bfloat16 on the way count: a program that leaves them out, or rounds other values in their place, can miss the bound.
Values may be sent and summed in bfloat16 or wider, within the bound.
A program may use at most 64 MiB of HBM per device.

v0:
```python
import jax
import jax.numpy as jnp
from jax import lax
from jax.sharding import PartitionSpec as P

UPDATES = 2


alpha_mix = 0.6
beta_keep = 0.9
step_size = 0.2
momentum_gain = 1.5
ridge_term = 1.0


def kernel_tile(left_rows, right_rows):
    inner_prod = lax.dot_general(
        left_rows, right_rows, (((1,), (1,)), ((), ())), preferred_element_type=jnp.float32
    )
    left_sq = jnp.sum(jnp.square(left_rows.astype(jnp.float32)), axis=1)
    right_sq = jnp.sum(jnp.square(right_rows.astype(jnp.float32)), axis=1)
    squared = left_sq[:, None] + right_sq[None, :] - 2.0 * inner_prod
    return jnp.exp(squared * (-3.5 / left_rows.shape[1])).astype(jnp.bfloat16)


def project_rows(factor, resid):
    return lax.dot_general(
        factor,
        resid.astype(jnp.bfloat16),
        (((0,), (0,)), ((), ())),
        preferred_element_type=jnp.float32,
    )


def finish_step(resid, factor, proj, core_now):
    lifted = jnp.dot(
        core_now, proj.astype(jnp.bfloat16), preferred_element_type=jnp.float32
    ).astype(jnp.bfloat16)
    return (resid - jnp.dot(factor, lifted, preferred_element_type=jnp.float32)).astype(
        jnp.bfloat16
    )


def owned_rows(local_feats, wanted, first_point):
    local_pos = wanted - first_point
    holder = (local_pos >= 0) & (local_pos < local_feats.shape[0])
    safe_pos = jnp.clip(local_pos, 0, local_feats.shape[0] - 1)
    return (holder, safe_pos)


def shards(features, targets, coefficients, momentum, block_index, pivot_index, nystrom_core):
    row_count = lax.axis_size("rows")
    pts_count = lax.axis_size("pts")
    row_id = lax.axis_index("rows")
    pts_id = lax.axis_index("pts")
    local_points = features.shape[0]
    per_row = block_index.shape[1] // row_count
    per_device = per_row // pts_count
    first_point = pts_id * local_points
    current = coefficients
    momentum_now = momentum
    for update in range(UPDATES):
        mixed = alpha_mix * momentum_now + (1.0 - alpha_mix) * current
        mixed_bf = mixed.astype(jnp.bfloat16)
        whole_index = block_index[update]
        row_points = lax.dynamic_slice_in_dim(whole_index, row_id * per_row, per_row)
        holder, safe_pos = owned_rows(features, row_points, first_point)
        row_terms = jnp.where(holder[:, None], features[safe_pos], jnp.zeros((), jnp.bfloat16))
        offset = jnp.where(
            holder[:, None],
            ridge_term * mixed[safe_pos] - targets[safe_pos].astype(jnp.float32),
            0.0,
        )
        pivot_points = whole_index[pivot_index[update]]
        pivot_holder, pivot_pos = owned_rows(features, pivot_points, first_point)
        pivot_terms = jnp.where(
            pivot_holder[:, None], features[pivot_pos], jnp.zeros((), jnp.bfloat16)
        )
        got_rows, got_pivots = (
            lax.psum(row_terms, "pts").astype(jnp.float32),
            lax.psum(pivot_terms, "pts").astype(jnp.float32),
        )
        block_feats = got_rows.astype(jnp.bfloat16)
        pivot_feats = got_pivots.astype(jnp.bfloat16)
        partial_value = (
            jnp.dot(
                kernel_tile(block_feats, features), mixed_bf, preferred_element_type=jnp.float32
            )
            + offset
        )
        local_all = whole_index - first_point
        whole_slots = jnp.where(
            (local_all >= 0) & (local_all < local_points), local_all, local_points
        )
        resid = lax.psum_scatter(partial_value, "pts", scatter_dimension=0, tiled=True)
        share_feats = lax.dynamic_slice_in_dim(block_feats, pts_id * per_device, per_device)
        factor = kernel_tile(share_feats, pivot_feats)
        proj = lax.psum(project_rows(factor, resid), ("rows", "pts"))
        step_bf = finish_step(resid, factor, proj, nystrom_core[update])
        steps = lax.all_gather(step_bf, ("rows", "pts"), axis=0, tiled=True)
        change = steps.astype(jnp.float32)
        current = mixed.at[whole_slots].add(-step_size * change, mode="drop")
        momentum_now = (
            (beta_keep * momentum_now + (1.0 - beta_keep) * mixed)
            .at[whole_slots]
            .add(-step_size * momentum_gain * change, mode="drop")
        )
    return (current, momentum_now)


def solution(mesh):
    in_specs = (P("pts", None), P("pts", None), P("pts", None), P("pts", None), P(), P(), P())
    out_specs = (P("pts", None), P("pts", None))
    return jax.shard_map(shards, mesh=mesh, in_specs=in_specs, out_specs=out_specs, check_vma=False)
```

profile of v0, /device:TPU:1, one launch (start us, length us, event | category | flops | bytes accessed | tf_op | source)
XLA Modules:
  0.0 1027.0 jit_solution(4563416117021022142)
XLA Ops:
  8.9 3.1 gather_fusion.8
  12.1 3.1 gather_fusion.3
  16.2 1.3 gather_fusion.4
  18.4 1.3 gather_fusion.9
  22.9 2.6 multiply_add_fusion.2
  26.4 1.2 gather_fusion.2
  27.8 140.3 %all-reduce.5.cloned.1.call-done = (bf16[256,128]{1,0:T(8,128)(2,1)}, bf16[512,128]{1,0:T(8,128)(2,1)}, bf16[256,128]{1,0:T(8,128)(2,1)}, bf16[512,128]{1,0:T(8,128)(2,1)}) async-done(((bf16[256,128]{1,0:T(8,128)(2,1)}, bf16[512,128]{1,0:T(8,128)(2,1)}, bf16[256,128]{1,0:T(8,128)(2,1)}, bf16[512,128]{1,0:T(8,128)(2,1)}), (bf16[256,128]{1,0:T(8,128)(2,1)}, bf16[512,128]{1,0:T(8,128)(2,1)}, ...) | async-done | bytes 393232 | tf_op jit(solution)/shard_map/psum | solution.py:80
  169.0 2.1 fusion.16
  173.0 210.5 %reduce-scatter.3.cloned.1.call-done = f32[8,256]{1,0:T(8,128)} async-done(((f32[256,256]{1,0:T(8,128)}), f32[8,256]{1,0:T(8,128)}) %reduce-scatter.3.cloned.1.call-update) | async-done | bytes 8208 | tf_op jit(solution)/shard_map/reduce_scatter | solution.py:95
  383.5 1.0 fusion.60
  384.6 83.0 %all-reduce.6 = bf16[512,256]{1,0:T(8,128)(2,1)S(1)} all-reduce(f32[512,256]{1,0:T(8,128)S(1)} %fusion.60), channel_id=1, replica_groups=mesh['rows'=8,'pts'=32] {'rows','pts'}, use_global_device_ids=true, to_apply=%region_7.8 | all-reduce | flops 131072 | bytes 786432 | tf_op jit(solution)/shard_map/psum | solution.py:98
  467.6 2.1 fusion.28
  469.8 1.2 gather_fusion.7
  471.1 98.4 %all-gather.3.cloned.1.call-done = bf16[2048,256]{1,0:T(8,128)(2,1)} async-done(((bf16[8,256]{1,0:T(8,128)(2,1)}), bf16[2048,256]{1,0:T(8,128)(2,1)}) %all-gather.3.cloned.1.call-update) | async-done | bytes 1048592 | tf_op jit(solution)/shard_map/all_gather | solution.py:100
  569.5 12.7 %scatter_custom_fusion.1 = f32[1024,256]{1,0:T(8,128)S(1)} fusion(f32[1024,256]{1,0:T(8,128)S(1)} %get-tuple-element.9, s32[2048]{0:T(1024)S(1)} %bitcast.54, bf16[2048,256]{1,0:T(8,128)(2,1)} %all-gather.3.cloned.1.call-done, f32[]{:T(128)} %constant.14.clone.1), kind=kCustom, calls=%fused_computation.19 | custom fusion | flops 1572864 | bytes 2097156 | tf_op jit(solution)/shard_map/scatter-add | solution.py:102
  582.2 13.8 %scatter_custom_fusion = f32[1024,256]{1,0:T(8,128)} fusion(f32[1024,256]{1,0:T(8,128)} %get-tuple-element.8, s32[2048]{0:T(1024)S(1)} %bitcast.55, bf16[2048,256]{1,0:T(8,128)(2,1)S(1)} %copy-done.3, f32[]{:T(128)} %constant.13.clone.1), kind=kCustom, calls=%fused_computation.18 | custom fusion | flops 1572864 | bytes 2097664 | tf_op jit(solution)/shard_map/scatter-add | solution.py:106
  596.0 2.5 multiply_add_fusion
  599.4 1.3 fusion.17
  601.2 206.7 %reduce-scatter.5.cloned.1.call-done = f32[8,256]{1,0:T(8,128)} async-done(((f32[256,256]{1,0:T(8,128)}), f32[8,256]{1,0:T(8,128)}) %reduce-scatter.5.cloned.1.call-update) | async-done | bytes 8208 | tf_op jit(solution)/shard_map/reduce_scatter | solution.py:95
  808.9 83.0 %all-reduce.7 = bf16[512,256]{1,0:T(8,128)(2,1)S(1)} all-reduce(f32[512,256]{1,0:T(8,128)S(1)} %fusion.58), channel_id=1, replica_groups=mesh['rows'=8,'pts'=32] {'rows','pts'}, use_global_device_ids=true, to_apply=%region_16.17 | all-reduce | flops 131072 | bytes 786432 | tf_op jit(solution)/shard_map/psum | solution.py:98
  892.0 2.1 fusion.29
  894.1 99.7 %all-gather.5.cloned.1.call-done = bf16[2048,256]{1,0:T(8,128)(2,1)} async-done(((bf16[8,256]{1,0:T(8,128)(2,1)}), bf16[2048,256]{1,0:T(8,128)(2,1)}) %all-gather.5.cloned.1.call-update) | async-done | bytes 1048592 | tf_op jit(solution)/shard_map/all_gather | solution.py:100
  993.8 12.5 %scatter_custom_fusion.2 = f32[1024,256]{1,0:T(8,128)S(1)} fusion(f32[1024,256]{1,0:T(8,128)S(1)} %get-tuple-element.7, s32[2048]{0:T(1024)S(1)} %bitcast.52, bf16[2048,256]{1,0:T(8,128)(2,1)} %all-gather.5.cloned.1.call-done, f32[]{:T(128)} %constant.14.clone.1), kind=kCustom, calls=%fused_computation.20 | custom fusion | flops 1572864 | bytes 2097156 | tf_op jit(solution)/shard_map/scatter-add | solution.py:102
  1006.3 14.1 %scatter_custom_fusion.3 = f32[1024,256]{1,0:T(8,128)} fusion(f32[1024,256]{1,0:T(8,128)} %get-tuple-element.6, s32[2048]{0:T(1024)S(1)} %bitcast.53, bf16[2048,256]{1,0:T(8,128)(2,1)S(1)} %copy-done.4, f32[]{:T(128)} %constant.13.clone.1), kind=kCustom, calls=%fused_computation.21 | custom fusion | flops 1572864 | bytes 2097664 | tf_op jit(solution)/shard_map/scatter-add | solution.py:106
  (67 shorter events, 13.3 us)
Async XLA Ops:
  7.2 19.2 %copy-start = (bf16[1024,256]{1,0:T(8,128)(2,1)S(1)}, bf16[1024,256]{1,0:T(8,128)(2,1)}, u32[]{:S(2)}) copy-start(bf16[1024,256]{1,0:T(8,128)(2,1)} %param.8) | copy-start | bytes 1572868
  7.2 160.9 %all-reduce.5.cloned.1.call-start = ((), (), s32[]{:S(2)}) async-start(), calls=%async_computation.6 | async-start | bytes 786432 | tf_op jit(solution)/shard_map/psum | solution.py:80
  12.1 3.2 copy-start.1
  18.4 4.5 copy-start.5
  22.8 360.7 %reduce-scatter.3.cloned.1.call-start = ((), (), s32[]{:S(2)}) async-start(), calls=%async_computation.2 | async-start | bytes 270336 | tf_op jit(solution)/shard_map/reduce_scatter | solution.py:95
  169.0 3.0 copy-start.7
  171.2 398.3 %all-gather.3.cloned.1.call-start = ((), (), s32[]{:S(2)}) async-start(), calls=%async_computation.3 | async-start | bytes 1052672 | tf_op jit(solution)/shard_map/all_gather | solution.py:100
  383.5 84.0 %copy-start.10 = (f32[8,256]{1,0:T(8,128)S(1)}, f32[8,256]{1,0:T(8,128)}, u32[]{:S(2)}) copy-start(f32[8,256]{1,0:T(8,128)} %reduce-scatter.3.cloned.1.call-done) | copy-start | bytes 24580
  467.5 3.4 copy-start.9
  467.5 3.4 copy-start.8
  469.7 338.1 %reduce-scatter.5.cloned.1.call-start = ((), (), s32[]{:S(2)}) async-start(), calls=%async_computation.4 | async-start | bytes 270336 | tf_op jit(solution)/shard_map/reduce_scatter | solution.py:95
  569.5 12.7 %copy-start.3 = (bf16[2048,256]{1,0:T(8,128)(2,1)S(1)}, bf16[2048,256]{1,0:T(8,128)(2,1)}, u32[]{:S(2)}) copy-start(bf16[2048,256]{1,0:T(8,128)(2,1)} %all-gather.3.cloned.1.call-done) | copy-start | bytes 3145732
  599.4 1.5 copy-start.6
  600.7 393.1 %all-gather.5.cloned.1.call-start = ((), (), s32[]{:S(2)}) async-start(), calls=%async_computation.5 | async-start | bytes 1052672 | tf_op jit(solution)/shard_map/all_gather | solution.py:100
  807.9 84.1 %copy-start.11 = (f32[8,256]{1,0:T(8,128)S(1)}, f32[8,256]{1,0:T(8,128)}, u32[]{:S(2)}) copy-start(f32[8,256]{1,0:T(8,128)} %reduce-scatter.5.cloned.1.call-done) | copy-start | bytes 24580
  993.8 12.5 %copy-start.4 = (bf16[2048,256]{1,0:T(8,128)(2,1)S(1)}, bf16[2048,256]{1,0:T(8,128)(2,1)}, u32[]{:S(2)}) copy-start(bf16[2048,256]{1,0:T(8,128)(2,1)} %all-gather.5.cloned.1.call-done) | copy-start | bytes 3145732
  1006.3 14.2 %copy-start.2 = (f32[1024,256]{1,0:T(8,128)}, f32[1024,256]{1,0:T(8,128)S(1)}, u32[]{:S(2)}) copy-start(f32[1024,256]{1,0:T(8,128)S(1)} %scatter_custom_fusion.2) | copy-start | bytes 3145732
Sparse Core Ops, SparseCore 0:
  22.9 145.1 all-reduce.4
  172.9 210.5 reduce-scatter.2
  469.8 99.5 all-gather.2
  600.8 206.9 reduce-scatter.4
  894.2 99.5 all-gather.4
where the time goes:
time: 1030 us
  waiting for transfers between devices  756 us (73%)
  blocking collectives  166 us (16%)
  other arithmetic  64.6 us (6%)
  local copies, waits for them, and re-layouts  15.8 us (2%)
  between operations  14.1 us (1%)
  matrix products  10.7 us (1%)
    reduce_scatter x2, waiting for transfers between devices, shards(): lax.psum_scatter(partial_value, 'pts', scatter_dimension=0, tiled=True)  417 us
    all_gather x2, waiting for transfers between devices, shards(): steps = lax.all_gather(step_bf, ('rows', 'pts'), axis=0, tiled=True)  198 us
    psum x2, blocking collectives, shards(): proj = lax.psum(project_rows(factor, resid), ('rows', 'pts'))  166 us
    psum x1, waiting for transfers between devices, shards(): lax.psum(row_terms, 'pts').astype(jnp.float32)  140 us
    scatter-add x2, other arithmetic, shards(): momentum_now = (beta_keep * momentum_now + (1.0 - beta_keep) * mixed).at[...  27.9 us
    scatter-add x2, other arithmetic, shards(): current = mixed.at[whole_slots].add(-step_size * change, mode='drop')  25.2 us
  transfers between devices with their start and end apart: 5, of which 5 were waited for; matrix products, arithmetic and copies ran while one was open for 1% of the time, Pallas kernels for 0%

commit v1 on v0

v1 whole, which is shorter than its diff:
```python
import functools

import jax
import jax.numpy as jnp
from jax import lax
from jax.experimental import pallas as pl
from jax.experimental.pallas import tpu as pltpu
from jax.sharding import PartitionSpec as P

alpha_mix = 0.6
beta_keep = 0.9
step_size = 0.2
momentum_gain = 1.5
ridge_term = 1.0

F32 = jnp.float32
BF16 = jnp.bfloat16
NN = (((1,), (0,)), ((), ()))
NT = (((1,), (1,)), ((), ()))
MESH = pl.DeviceIdType.MESH

PTS = 32
ROWS = 8
LOCAL = 1024
GROUP = 256
SLOTS = 32


def dot(left, right, dims=NN):
    return lax.dot_general(left, right, dims, preferred_element_type=F32)


def row_norms(rows):
    squares = jnp.square(rows.astype(F32))
    high = squares.astype(BF16)
    low = (squares - high.astype(F32)).astype(BF16)
    ones = jnp.ones((8, rows.shape[1]), BF16)
    return dot(ones, high, NT) + dot(ones, low, NT)


def kernel_tile(left, right, right_sq):
    scale = -3.5 / left.shape[1]
    left_sq = jnp.sum(jnp.square(left.astype(F32)), axis=1, keepdims=True)
    squared = left_sq + right_sq - 2.0 * dot(left, right, NT)
    return jnp.exp(squared * scale).astype(BF16)


def iota(shape, axis):
    return lax.broadcasted_iota(jnp.int32, shape, axis).astype(F32)


def owner_of(index):
    return jnp.floor(index * (1.0 / LOCAL))


def mod4(value):
    return value - 4.0 * jnp.floor(value * 0.25)


def stack(value):
    return jnp.concatenate([value[:, :128], value[:, 128:]], axis=0)


def unstack(value):
    return [value[:8], value[8:]]


def block_kernel(
    bi_ref, pv_ref, x_ref, w_hbm, z_hbm, t_hbm, core_hbm,
    steps_ref, places_ref,
    idx_ref, idxt_ref, w_ref, z_ref, t_ref, core_ref, load_sem,
    sel_ref, g_snd, g_rcv, feats_ref, factor_ref, cross_ref, mixb_ref, baseb_ref,
    off_ref, baserow_ref, rs0_snd, rs0_rcv, rs1_snd, rs1_rcv, ax_ref, d_snd, d_rcv,
    send_sem, recv_sem,
):
    me_r = lax.axis_index("rows")
    me_p = lax.axis_index("pts")
    core = lax.rem(me_r, 2)
    chip = me_r // 2
    p_f = me_p.astype(F32)
    r_f = me_r.astype(F32)

    barrier = pltpu.get_barrier_semaphore()

    def greet_pts(hop, carry):
        pl.semaphore_signal(
            barrier, inc=1, device_id={"pts": lax.rem(me_p + hop, PTS)}, device_id_type=MESH
        )
        return carry

    def greet_rows(hop, carry):
        pl.semaphore_signal(
            barrier, inc=1, device_id={"rows": lax.rem(me_r + hop, ROWS)}, device_id_type=MESH
        )
        return carry

    lax.fori_loop(1, PTS, greet_pts, 0)
    lax.fori_loop(1, ROWS, greet_rows, 0)

    loads = [
        pltpu.make_async_copy(src, dst, load_sem.at[at])
        for at, (src, dst) in enumerate(
            [(w_hbm, w_ref), (z_hbm, z_ref), (t_hbm, t_ref), (core_hbm, core_ref)]
        )
    ]
    for load in loads:
        load.start()

    def wait_bytes(ref, sem):
        pltpu.make_async_copy(ref, ref, sem).wait()

    idx_ref[...] = jnp.zeros_like(idx_ref)
    for update in range(2):
        for group in range(ROWS):
            at = update * ROWS + group
            idx_ref[at : at + 1, :] = bi_ref[
                update : update + 1, group * GROUP : (group + 1) * GROUP
            ].astype(F32)
        own = pl.ds(pl.multiple_of(me_r * GROUP, GROUP), GROUP)
        idx_ref[16 + update : 17 + update, :] = bi_ref[update : update + 1, own].astype(F32)
        for half in range(2):
            at = 18 + update * 2 + half
            idx_ref[at : at + 1, :] = pv_ref[
                update : update + 1, half * GROUP : (half + 1) * GROUP
            ].astype(F32)
    idxt_ref[...] = jnp.transpose(idx_ref[...])

    below = iota((GROUP, GROUP), 1) < iota((GROUP, GROUP), 0)
    above = iota((GROUP, GROUP), 0) < iota((GROUP, GROUP), 1)
    ones_mat = jnp.ones((GROUP, 128), BF16)

    def owners(at):
        return owner_of(idxt_ref[:, at : at + 1]), owner_of(idx_ref[at : at + 1, :])

    def rank_col(at):
        col, row = owners(at)
        same = jnp.where((col == row) & below, 1.0, 0.0).astype(BF16)
        return dot(same, ones_mat)

    def rank_row(at):
        col, row = owners(at)
        same = jnp.where((col == row) & above, 1.0, 0.0).astype(BF16)
        return dot(jnp.ones((8, GROUP), BF16), same)

    for update in range(2):
        row = idx_ref[16 + update : 17 + update, :]
        rank = rank_row(16 + update)[0:1]
        slot = jnp.where(owner_of(row) == p_f, rank, -1.0)
        pick = jnp.where(iota((SLOTS, GROUP), 0) == slot, 1.0, 0.0).astype(BF16)
        col = idxt_ref[:, 16 + update : 17 + update] - p_f * LOCAL
        hot = jnp.where(iota((GROUP, LOCAL), 1) == col, 1.0, 0.0).astype(BF16)
        place = dot(pick, hot).astype(BF16)
        g_snd[update] = dot(place, x_ref[...]).astype(BF16)

    pl.semaphore_wait(barrier, PTS + ROWS - 2)

    def to_pts(src_of, dst, sem):
        def send(hop, carry):
            peer = lax.rem(me_p + hop, PTS)
            pltpu.make_async_remote_copy(
                src_ref=src_of(peer), dst_ref=dst.at[me_p],
                send_sem=send_sem.at[sem], recv_sem=recv_sem.at[sem],
                device_id={"pts": peer}, device_id_type=MESH,
            ).start()
            return carry

        lax.fori_loop(1, PTS, send, 0)

    def to_rows(buf, sem):
        def send(hop, carry):
            peer = lax.rem(me_r + hop, ROWS)
            pltpu.make_async_remote_copy(
                src_ref=buf.at[me_r], dst_ref=buf.at[me_r],
                send_sem=send_sem.at[sem], recv_sem=recv_sem.at[sem],
                device_id={"rows": peer}, device_id_type=MESH,
            ).start()
            return carry

        lax.fori_loop(1, ROWS, send, 0)

    G, RS0, RS1, AX, DS, FX, FC = 0, 2, 3, 4, 7, 9, 11
    for update in range(2):
        to_pts(lambda peer: g_snd.at[update], g_rcv.at[update], G + update)
        g_rcv[update, me_p] = g_snd[update]

    loads[0].wait()
    loads[1].wait()
    w_now = w_ref[...]
    z_now = z_ref[...]
    mixed = alpha_mix * z_now + (1.0 - alpha_mix) * w_now
    base = alpha_mix * (beta_keep * z_now + (1.0 - beta_keep) * mixed) + (1.0 - alpha_mix) * mixed
    mixb_ref[...] = mixed.astype(BF16)
    baseb_ref[...] = base.astype(BF16)
    loads[2].wait()
    targets = t_ref[...].astype(F32)
    for update, value in enumerate((mixed, base)):
        wanted = ridge_term * value - targets
        high = wanted.astype(BF16)
        low = (wanted - high.astype(F32)).astype(BF16)
        col = idxt_ref[:, 16 + update : 17 + update] - p_f * LOCAL
        hot = jnp.where(iota((GROUP, LOCAL), 1) == col, 1.0, 0.0).astype(BF16)
        off_ref[update] = dot(hot, high) + dot(hot, low)
        if update == 0:
            baserow_ref[...] = dot(hot, baseb_ref[...])

    x_sq = row_norms(x_ref[...])[0:1]

    def select_group(at, group_f, update):
        col = owner_of(idxt_ref[:, at : at + 1])
        quad = jnp.floor(col * 0.25)
        chunk = mod4(col - 4.0 * quad + group_f)
        slot = rank_col(at) + (quad * 128.0 + chunk * SLOTS)
        for block in range(ROWS):
            hit = iota((GROUP, 128), 1) + 128.0 * block == slot
            sel_ref[at, :, block * 128 : (block + 1) * 128] = jnp.where(hit, 1.0, 0.0).astype(BF16)

    for update in range(2):
        for group in range(ROWS):
            select_group(update * ROWS + group, float(group), update)

    my_quad = me_p // 4
    my_kind = p_f - 4.0 * my_quad.astype(F32)
    chunk_of = jnp.floor(iota((8, 128), 1) * (1.0 / SLOTS))
    places_ref[...] = jnp.zeros_like(places_ref)
    for update in range(2):
        for half in range(2):
            total = jnp.zeros((8, 128), F32)
            for part in range(4):
                group = half * 4 + part
                at = update * ROWS + group
                row = idx_ref[at : at + 1, :]
                inner = row - LOCAL * owner_of(row)
                upper = jnp.floor(inner * (1.0 / 32.0))
                lhs = jnp.concatenate(
                    [upper, inner - 32.0 * upper, jnp.ones_like(row), jnp.zeros((5, GROUP), F32)],
                    axis=0,
                ).astype(BF16)
                block = sel_ref[at, :, pl.ds(pl.multiple_of(my_quad * 128, 128), 128)]
                found = dot(lhs, block)
                total = jnp.where(chunk_of == mod4(my_kind + part), found, total)
            point = 32.0 * total[0:1] + total[1:2] - (1.0 - total[2:3])
            places_ref[update : update + 1, half * 128 : (half + 1) * 128] = point

    slots_iota = iota((GROUP, PTS * SLOTS), 1)

    def own_features(update):
        wait_bytes(g_rcv.at[update, pl.ds(0, PTS - 1)], recv_sem.at[G + update])
        col = owner_of(idxt_ref[:, 16 + update : 17 + update])
        slot = rank_col(16 + update)[:, 0:1] + col * SLOTS
        hot = jnp.where(slots_iota == slot, 1.0, 0.0).astype(BF16)
        rows = dot(hot, g_rcv[update].reshape(PTS * SLOTS, 128)).astype(BF16)
        feats_ref[update, core, chip] = rows
        for hop in range(1, 4):
            pltpu.make_async_remote_copy(
                src_ref=feats_ref.at[update, core, chip],
                dst_ref=feats_ref.at[update, core, chip],
                send_sem=send_sem.at[FX + update], recv_sem=recv_sem.at[FX + update],
                device_id={"rows": lax.rem(me_r + 2 * hop, ROWS)}, device_id_type=MESH,
            ).start()
        return rows

    def share_with_core(update):
        wait_bytes(feats_ref.at[update, core, pl.ds(0, 3)], recv_sem.at[FX + update])
        pltpu.make_async_remote_copy(
            src_ref=feats_ref.at[update, core], dst_ref=feats_ref.at[update, core],
            send_sem=send_sem.at[FC + update], recv_sem=recv_sem.at[FC + update],
            device_id={"rows": chip * 2 + 1 - core}, device_id_type=MESH,
        ).start()

    def group_rows(update, group):
        return feats_ref[update, lax.rem(group, 2), group // 2]

    def partial_rows(rows, coefs, offset):
        tile = kernel_tile(rows, x_ref[...], x_sq)
        return dot(tile, coefs) + offset

    def put_pieces(dst, value, lead):
        flipped = jnp.transpose(value)
        for piece in range(PTS):
            dst[piece, lead : lead + 16, :] = stack(
                flipped[piece * 8 : piece * 8 + 8]
            ).astype(BF16)

    rows0 = own_features(0)
    put_pieces(rs0_snd, partial_rows(rows0, mixb_ref[...], off_ref[0]), 0)
    to_pts(lambda peer: rs0_snd.at[peer], rs0_rcv, RS0)
    rs0_rcv[me_p] = rs0_snd[me_p]

    rows1 = own_features(1)
    put_pieces(rs1_snd, partial_rows(rows1, baseb_ref[...], off_ref[1]), 0)
    put_pieces(rs1_snd, baserow_ref[...], 16)
    to_pts(lambda peer: rs1_snd.at[peer], rs1_rcv, RS1)
    rs1_rcv[me_p] = rs1_snd[me_p]

    def make_factor(update):
        share_with_core(update)
        wait_bytes(feats_ref.at[update, core], recv_sem.at[FC + update])
        pivots = []
        for half in range(2):
            at = 18 + update * 2 + half
            col = idxt_ref[:, at : at + 1]
            total = jnp.zeros((GROUP, 128), F32)
            for group in range(ROWS):
                hot = jnp.where(iota((GROUP, GROUP), 1) + float(group * GROUP) == col, 1.0, 0.0)
                total = total + dot(hot.astype(BF16), feats_ref[update, group % 2, group // 2])
            pivots.append(total.astype(BF16))
        pivots = jnp.concatenate(pivots, axis=0)
        pivots_sq = row_norms(pivots)[0:1]

        def body(group, carry):
            at = pl.ds(pl.multiple_of(group * GROUP, GROUP), GROUP)
            factor_ref[update, at, :] = kernel_tile(group_rows(update, group), pivots, pivots_sq)
            return carry

        lax.fori_loop(0, ROWS, body, 0)

    make_factor(0)
    rows1_sq = row_norms(rows1)[0:1]
    row1 = idx_ref[17:18, :]
    for group in range(ROWS):
        tile = kernel_tile(feats_ref[0, group % 2, group // 2], rows1, rows1_sq)
        same = jnp.where(idxt_ref[:, group : group + 1] == row1, ridge_term, 0.0)
        cross_ref[group * GROUP : (group + 1) * GROUP, :] = (tile.astype(F32) + same).astype(BF16)

    def sum_pieces(rcv, lead):
        total = rcv[0, lead : lead + 16, :].astype(F32)
        for piece in range(1, PTS):
            total = total + rcv[piece, lead : lead + 16, :].astype(F32)
        return total

    def share_rows(at, value):
        ax_ref[at, me_r] = value.astype(BF16)
        to_rows(ax_ref.at[at], AX + at)

    def whole_rows(at):
        wait_bytes(ax_ref.at[at, pl.ds(0, ROWS - 1)], recv_sem.at[AX + at])
        parts = []
        for group in range(ROWS):
            parts += unstack(ax_ref[at, group].astype(F32))
        return jnp.concatenate(parts, axis=1)

    wait_bytes(rs0_rcv.at[pl.ds(0, PTS - 1)], recv_sem.at[RS0])
    share_rows(0, sum_pieces(rs0_rcv, 0))
    wait_bytes(rs1_rcv.at[pl.ds(0, PTS - 1)], recv_sem.at[RS1])
    share_rows(1, sum_pieces(rs1_rcv, 16))
    partial1 = sum_pieces(rs1_rcv, 0)
    make_factor(1)
    loads[3].wait()

    def step_of(update, resid):
        proj = dot(resid.astype(BF16), factor_ref[update])
        lifted = dot(proj.astype(BF16), core_ref[update], NT).astype(BF16)
        return (resid - dot(lifted, factor_ref[update], NT)).astype(BF16)

    def send_steps(update, step):
        chunk_at = jnp.floor(iota((8, 128), 1) * (1.0 / SLOTS))
        for half in range(2):
            found = []
            for part in range(4):
                group = half * 4 + part
                found.append(
                    dot(step[:, group * GROUP : (group + 1) * GROUP], sel_ref[update * ROWS + group])
                )
            for owner in range(PTS):
                block = owner // 4
                kind = owner % 4
                total = jnp.zeros((8, 128), F32)
                for part in range(4):
                    piece = found[part][:, block * 128 : (block + 1) * 128]
                    total = jnp.where(chunk_at == float((kind + part) % 4), piece, total)
                d_snd[update, owner, half] = total
        for owner in range(PTS):
            d_out = jnp.concatenate([d_snd[update, owner, 0], d_snd[update, owner, 1]], axis=0)
            d_rcv[2 + update, owner] = d_out.astype(BF16)
        to_pts(lambda peer: d_rcv.at[2 + update, peer], d_rcv.at[update], DS + update)
        d_rcv[update, me_p] = d_rcv[2 + update, me_p]

    resid0 = whole_rows(0)
    step0 = step_of(0, resid0)
    base_rows = whole_rows(1)
    drop = alpha_mix * step_size * momentum_gain + (1.0 - alpha_mix) * step_size
    moved = (base_rows - drop * step0.astype(F32)).astype(BF16).astype(F32) - base_rows
    high = moved.astype(BF16)
    low = (moved - high.astype(F32)).astype(BF16)
    lhs = jnp.concatenate([high.astype(F32), low.astype(F32)], axis=0).astype(BF16)
    change = dot(lhs, cross_ref[...])
    share_rows(2, partial1 + stack(change[:8] + change[8:]))
    send_steps(0, step0)
    step1 = step_of(1, whole_rows(2))
    send_steps(1, step1)

    for update in range(2):
        wait_bytes(d_rcv.at[update, pl.ds(0, PTS - 1)], recv_sem.at[DS + update])
        steps_ref[update] = d_rcv[update]

    for update in range(2):
        wait_bytes(g_rcv.at[update, pl.ds(0, PTS - 1)], send_sem.at[G + update])
        wait_bytes(feats_ref.at[update, core, pl.ds(0, 3)], send_sem.at[FX + update])
        wait_bytes(feats_ref.at[update, core], send_sem.at[FC + update])
        wait_bytes(d_rcv.at[update, pl.ds(0, PTS - 1)], send_sem.at[DS + update])
    wait_bytes(rs0_rcv.at[pl.ds(0, PTS - 1)], send_sem.at[RS0])
    wait_bytes(rs1_rcv.at[pl.ds(0, PTS - 1)], send_sem.at[RS1])
    for at in range(3):
        wait_bytes(ax_ref.at[at, pl.ds(0, ROWS - 1)], send_sem.at[AX + at])


def apply_kernel(w_ref, z_ref, steps_ref, places_ref, w_out, z_out):
    rows = w_ref.shape[0]
    first = (pl.program_id(0) * rows).astype(F32)

    def change(update):
        halves = []
        for half in range(2):
            cut = slice(half * 8, half * 8 + 8)
            halves.append(
                jnp.concatenate(
                    [steps_ref[update, piece].astype(F32)[cut] for piece in range(PTS)], axis=0
                )
            )
        steps = jnp.concatenate(halves, axis=1).astype(BF16)
        place = places_ref[update : update + 1, :]
        hot = jnp.where(iota((rows, GROUP), 0) + first == place, 1.0, 0.0).astype(BF16)
        return dot(hot, steps, NT)

    current = w_ref[...]
    momentum_now = z_ref[...]
    for update in range(2):
        delta = change(update)
        mixed = alpha_mix * momentum_now + (1.0 - alpha_mix) * current
        current = mixed - step_size * delta
        momentum_now = (
            beta_keep * momentum_now + (1.0 - beta_keep) * mixed
        ) - step_size * momentum_gain * delta
    w_out[...] = current
    z_out[...] = momentum_now


def shards(features, targets, coefficients, momentum, block_index, pivot_index, nystrom_core):
    vmem = pl.BlockSpec(memory_space=pltpu.VMEM)
    anywhere = pl.BlockSpec(memory_space=pl.ANY)
    steps, places = pl.pallas_call(
        block_kernel,
        out_shape=(
            jax.ShapeDtypeStruct((2, PTS, 16, 128), BF16),
            jax.ShapeDtypeStruct((8, GROUP), F32),
        ),
        in_specs=[vmem, vmem, vmem, anywhere, anywhere, anywhere, anywhere],
        out_specs=(vmem, vmem),
        scratch_shapes=[
            pltpu.VMEM((128, GROUP), F32),
            pltpu.VMEM((GROUP, 128), F32),
            pltpu.VMEM((LOCAL, 256), F32),
            pltpu.VMEM((LOCAL, 256), F32),
            pltpu.VMEM((LOCAL, 256), BF16),
            pltpu.VMEM((2, 512, 512), BF16),
            pltpu.SemaphoreType.DMA((4,)),
            pltpu.VMEM((16, GROUP, PTS * SLOTS), BF16),
            pltpu.VMEM((2, SLOTS, 128), BF16),
            pltpu.VMEM((2, PTS, SLOTS, 128), BF16),
            pltpu.VMEM((2, 2, 4, GROUP, 128), BF16),
            pltpu.VMEM((2, ROWS * GROUP, 512), BF16),
            pltpu.VMEM((ROWS * GROUP, GROUP), BF16),
            pltpu.VMEM((LOCAL, 256), BF16),
            pltpu.VMEM((LOCAL, 256), BF16),
            pltpu.VMEM((2, GROUP, 256), F32),
            pltpu.VMEM((GROUP, 256), F32),
            pltpu.VMEM((PTS, 16, 128), BF16),
            pltpu.VMEM((PTS, 16, 128), BF16),
            pltpu.VMEM((PTS, 32, 128), BF16),
            pltpu.VMEM((PTS, 32, 128), BF16),
            pltpu.VMEM((3, ROWS, 16, 128), BF16),
            pltpu.VMEM((2, PTS, 2, 8, 128), F32),
            pltpu.VMEM((4, PTS, 16, 128), BF16),
            pltpu.SemaphoreType.DMA((13,)),
            pltpu.SemaphoreType.DMA((13,)),
        ],
        compiler_params=pltpu.CompilerParams(
            collective_id=0, has_side_effects=True, vmem_limit_bytes=56 * 1024 * 1024
        ),
        name="block_steps",
    )(block_index, pivot_index, features, coefficients, momentum, targets, nystrom_core)

    tile = 256
    by_rows = pl.BlockSpec((tile, 256), lambda at: (at, 0))
    return pl.pallas_call(
        apply_kernel,
        grid=(LOCAL // tile,),
        out_shape=(
            jax.ShapeDtypeStruct(coefficients.shape, F32),
            jax.ShapeDtypeStruct(momentum.shape, F32),
        ),
        in_specs=[
            by_rows,
            by_rows,
            pl.BlockSpec((2, PTS, 16, 128), lambda at: (0, 0, 0, 0)),
            pl.BlockSpec((8, GROUP), lambda at: (0, 0)),
        ],
        out_specs=(by_rows, by_rows),
        name="apply_steps",
    )(coefficients, momentum, steps, places)


def solution(mesh):
    in_specs = (P("pts", None), P("pts", None), P("pts", None), P("pts", None), P(), P(), P())
    out_specs = (P("pts", None), P("pts", None))
    return jax.shard_map(shards, mesh=mesh, in_specs=in_specs, out_specs=out_specs, check_vma=False)
```

time: 1030 us -> 60.4 us (0.06)
  waiting for transfers between devices: 756 us -> 0 us
  blocking collectives: 166 us -> 0 us
  other arithmetic: 64.6 us -> 0 us
  Pallas kernels: 0 us -> 59.6 us
  local copies, waits for them, and re-layouts: 15.8 us -> 0 us
  between operations: 14.1 us -> 0.64 us
  matrix products: 10.7 us -> 0 us
    reduce_scatter x2 -> x0, waiting for transfers between devices: 417 us -> none  [shards(): lax.psum_scatter(partial_value, 'pts', scatter_dimension=0, tiled=True)]
    all_gather x2 -> x0, waiting for transfers between devices: 198 us -> none  [shards(): steps = lax.all_gather(step_bf, ('rows', 'pts'), axis=0, tiled=True)]
    psum x2 -> x0, blocking collectives: 166 us -> none  [shards(): proj = lax.psum(project_rows(factor, resid), ('rows', 'pts'))]
    psum x1 -> x0, waiting for transfers between devices: 140 us -> none  [shards(): lax.psum(row_terms, 'pts').astype(jnp.float32)]
    pallas_call x0 -> x2, Pallas kernels: none -> 59.6 us  [the longest x1 55.1 us: shards(): pl.pallas_call(block_kernel, out_shape=(jax.ShapeDtypeStruct((2, PTS, 16,...]
    scatter-add x4 -> x0, other arithmetic: 53.1 us -> none  [the longest x2 27.9 us: shards(): momentum_now = (beta_keep * momentum_now + (1.0 - beta_keep) * mixed).at[...]
    gather x10 -> x0, local copies, waits for them, and re-layouts: 14.9 us -> none  [the longest x2 6.29 us: shards(): pivot_points = whole_index[pivot_index[update]]]
    dot_general x8 -> x0, matrix products: 10.7 us -> none  [the longest x2 4.25 us: finish_step(): jnp.dot(factor, lifted, preferred_element_type=jnp.float32)]
  transfers between devices with their start and end apart: 5 -> 0, of which waited for: 5 -> 0; matrix products, arithmetic and copies ran while one was open for 1% -> 0% of each run, Pallas kernels for 0% -> 0%
where the time goes in v1:
time: 60.4 us; the launch traced here: 60.2 us
  Pallas kernels  59.6 us (99%)
  between operations  0.64 us (1%)
    pallas_call x1, Pallas kernels, shards(): pl.pallas_call(block_kernel, out_shape=(jax.ShapeDtypeStruct((2, PTS, 16,...  55.1 us
    pallas_call x1, Pallas kernels, shards(): pl.pallas_call(apply_kernel, grid=(LOCAL // tile,), out_shape=(jax.ShapeD...  4.47 us

profile of v1, /device:TPU:1, one launch (start us, length us, event | category | flops | bytes accessed | tf_op | source)
XLA Modules:
  0.0 60.2 jit_solution(1707224064894575201)
XLA Ops:
  0.6 55.1 %block_steps.1 = (bf16[2,32,16,128]{3,2,1,0:T(8,128)(2,1)}, f32[8,256]{1,0:T(8,128)}) custom-call(s32[2,2048]{1,0:T(2,128)} %bi_ref.1, s32[2,512]{1,0:T(2,128)} %pv_ref.1, bf16[1024,128]{1,0:T(8,128)(2,1)} %x_ref.1, f32[1024,256]{1,0:T(8,128)} %w_ref.1, f32[1024,256]{1,0:T(8,128)} %z_ref.1, bf16[1024,256]{1,0:T(8,128)(2,1)} %t_hbm.1, ...), custom_call_target="tpu_custom_call" | custom-call | tf_op jit(solution)/shard_map/block_steps/pallas_call | solution.py:441
  55.7 4.5 %apply_steps.1 = (f32[1024,256]{1,0:T(8,128)}, f32[1024,256]{1,0:T(8,128)}) custom-call(f32[1024,256]{1,0:T(8,128)} %w_ref.1, f32[1024,256]{1,0:T(8,128)} %z_ref.1, bf16[2,32,16,128]{3,2,1,0:T(8,128)(2,1)} %get-tuple-element.4.steps_ref, f32[8,256]{1,0:T(8,128)} %get-tuple-element.5.places_ref), custom_call_target="tpu_custom_call" | custom-call | tf_op jit(solution)/shard_map/apply_steps/pallas_call | solution.py:485

commit v2 on v1

--- a/solution.py
+++ b/solution.py
@@ -23,6 +23,7 @@
 ROWS = 8
 LOCAL = 1024
 GROUP = 256
+CAP = 24
 SLOTS = 32
 
 
@@ -65,12 +66,23 @@
     return [value[:8], value[8:]]
 
 
+def apply_update(current, momentum_now, steps, place, first):
+    hot = jnp.where(iota((current.shape[0], GROUP), 0) + first == place, 1.0, 0.0).astype(BF16)
+    delta = dot(hot, steps, NT)
+    mixed = alpha_mix * momentum_now + (1.0 - alpha_mix) * current
+    current = mixed - step_size * delta
+    momentum_now = (
+        beta_keep * momentum_now + (1.0 - beta_keep) * mixed
+    ) - step_size * momentum_gain * delta
+    return current, momentum_now
+
+
 def block_kernel(
     bi_ref, pv_ref, x_ref, w_hbm, z_hbm, t_hbm, core_hbm,
-    steps_ref, places_ref,
+    w_mid, z_mid, steps_ref, places_ref,
     idx_ref, idxt_ref, w_ref, z_ref, t_ref, core_ref, load_sem,
     sel_ref, g_snd, g_rcv, feats_ref, factor_ref, cross_ref, mixb_ref, baseb_ref,
-    off_ref, baserow_ref, rs0_snd, rs0_rcv, rs1_snd, rs1_rcv, ax_ref, d_snd, d_rcv,
+    off_ref, rs0_snd, rs0_rcv, rs1_snd, rs1_rcv, ax_ref, d_snd, d_rcv,
     send_sem, recv_sem,
 ):
     me_r = lax.axis_index("rows")
@@ -108,6 +120,16 @@
 
     def wait_bytes(ref, sem):
         pltpu.make_async_copy(ref, ref, sem).wait()
+
+    arrivals = {}
+    sent = []
+
+    def expect(sem, ref):
+        arrivals[sem] = ref
+        sent.append((sem, ref))
+
+    def arrive(sem):
+        wait_bytes(arrivals.pop(sem), recv_sem.at[sem])
 
     idx_ref[...] = jnp.zeros_like(idx_ref)
     for update in range(2):
@@ -146,7 +168,7 @@
         row = idx_ref[16 + update : 17 + update, :]
         rank = rank_row(16 + update)[0:1]
         slot = jnp.where(owner_of(row) == p_f, rank, -1.0)
-        pick = jnp.where(iota((SLOTS, GROUP), 0) == slot, 1.0, 0.0).astype(BF16)
+        pick = jnp.where(iota((CAP, GROUP), 0) == slot, 1.0, 0.0).astype(BF16)
         col = idxt_ref[:, 16 + update : 17 + update] - p_f * LOCAL
         hot = jnp.where(iota((GROUP, LOCAL), 1) == col, 1.0, 0.0).astype(BF16)
         place = dot(pick, hot).astype(BF16)
@@ -165,6 +187,7 @@
             return carry
 
         lax.fori_loop(1, PTS, send, 0)
+        expect(sem, dst.at[pl.ds(0, PTS - 1)])
 
     def to_rows(buf, sem):
         def send(hop, carry):
@@ -177,8 +200,9 @@
             return carry
 
         lax.fori_loop(1, ROWS, send, 0)
-
-    G, RS0, RS1, AX, DS, FX, FC = 0, 2, 3, 4, 7, 9, 11
+        expect(sem, buf.at[pl.ds(0, ROWS - 1)])
+
+    G, RS0, RS1, AX, DS, FX, FC = 0, 2, 3, 4, 6, 8, 10
     for update in range(2):
         to_pts(lambda peer: g_snd.at[update], g_rcv.at[update], G + update)
         g_rcv[update, me_p] = g_snd[update]
@@ -200,8 +224,6 @@
         col = idxt_ref[:, 16 + update : 17 + update] - p_f * LOCAL
         hot = jnp.where(iota((GROUP, LOCAL), 1) == col, 1.0, 0.0).astype(BF16)
         off_ref[update] = dot(hot, high) + dot(hot, low)
-        if update == 0:
-            baserow_ref[...] = dot(hot, baseb_ref[...])
 
     x_sq = row_norms(x_ref[...])[0:1]
 
@@ -241,14 +263,14 @@
             point = 32.0 * total[0:1] + total[1:2] - (1.0 - total[2:3])
             places_ref[update : update + 1, half * 128 : (half + 1) * 128] = point
 
-    slots_iota = iota((GROUP, PTS * SLOTS), 1)
+    slots_iota = iota((GROUP, PTS * CAP), 1)
 
     def own_features(update):
-        wait_bytes(g_rcv.at[update, pl.ds(0, PTS - 1)], recv_sem.at[G + update])
+        arrive(G + update)
         col = owner_of(idxt_ref[:, 16 + update : 17 + update])
-        slot = rank_col(16 + update)[:, 0:1] + col * SLOTS
+        slot = rank_col(16 + update)[:, 0:1] + col * CAP
         hot = jnp.where(slots_iota == slot, 1.0, 0.0).astype(BF16)
-        rows = dot(hot, g_rcv[update].reshape(PTS * SLOTS, 128)).astype(BF16)
+        rows = dot(hot, g_rcv[update].reshape(PTS * CAP, 128)).astype(BF16)
         feats_ref[update, core, chip] = rows
         for hop in range(1, 4):
             pltpu.make_async_remote_copy(
@@ -257,15 +279,17 @@
                 send_sem=send_sem.at[FX + update], recv_sem=recv_sem.at[FX + update],
                 device_id={"rows": lax.rem(me_r + 2 * hop, ROWS)}, device_id_type=MESH,
             ).start()
+        expect(FX + update, feats_ref.at[update, core, pl.ds(0, 3)])
         return rows
 
     def share_with_core(update):
-        wait_bytes(feats_ref.at[update, core, pl.ds(0, 3)], recv_sem.at[FX + update])
+        arrive(FX + update)
         pltpu.make_async_remote_copy(
             src_ref=feats_ref.at[update, core], dst_ref=feats_ref.at[update, core],
             send_sem=send_sem.at[FC + update], recv_sem=recv_sem.at[FC + update],
             device_id={"rows": chip * 2 + 1 - core}, device_id_type=MESH,
         ).start()
+        expect(FC + update, feats_ref.at[update, core])
 
     def group_rows(update, group):
         return feats_ref[update, lax.rem(group, 2), group // 2]
@@ -274,27 +298,23 @@
         tile = kernel_tile(rows, x_ref[...], x_sq)
         return dot(tile, coefs) + offset
 
-    def put_pieces(dst, value, lead):
+    def put_pieces(dst, value):
         flipped = jnp.transpose(value)
         for piece in range(PTS):
-            dst[piece, lead : lead + 16, :] = stack(
-                flipped[piece * 8 : piece * 8 + 8]
-            ).astype(BF16)
+            dst[piece] = stack(flipped[piece * 8 : piece * 8 + 8]).astype(BF16)
 
     rows0 = own_features(0)
-    put_pieces(rs0_snd, partial_rows(rows0, mixb_ref[...], off_ref[0]), 0)
+    put_pieces(rs0_snd, partial_rows(rows0, mixb_ref[...], off_ref[0]))
     to_pts(lambda peer: rs0_snd.at[peer], rs0_rcv, RS0)
     rs0_rcv[me_p] = rs0_snd[me_p]
 
     rows1 = own_features(1)
-    put_pieces(rs1_snd, partial_rows(rows1, baseb_ref[...], off_ref[1]), 0)
-    put_pieces(rs1_snd, baserow_ref[...], 16)
+    put_pieces(rs1_snd, partial_rows(rows1, baseb_ref[...], off_ref[1]))
     to_pts(lambda peer: rs1_snd.at[peer], rs1_rcv, RS1)
     rs1_rcv[me_p] = rs1_snd[me_p]
 
     def make_factor(update):
-        share_with_core(update)
-        wait_bytes(feats_ref.at[update, core], recv_sem.at[FC + update])
+        arrive(FC + update)
         pivots = []
         for half in range(2):
             at = 18 + update * 2 + half
@@ -314,37 +334,34 @@
 
         lax.fori_loop(0, ROWS, body, 0)
 
+    def sum_pieces(rcv):
+        total = rcv[0].astype(F32)
+        for piece in range(1, PTS):
+            total = total + rcv[piece].astype(F32)
+        return total
+
+    def share_rows(at, value):
+        ax_ref[at, me_r] = value.astype(BF16)
+        to_rows(ax_ref.at[at], AX + at)
+
+    def whole_rows(at):
+        arrive(AX + at)
+        parts = []
+        for group in range(ROWS):
+            parts += unstack(ax_ref[at, group].astype(F32))
+        return jnp.concatenate(parts, axis=1)
+
+    share_with_core(0)
+    arrive(RS0)
+    share_rows(0, sum_pieces(rs0_rcv))
     make_factor(0)
+    share_with_core(1)
     rows1_sq = row_norms(rows1)[0:1]
     row1 = idx_ref[17:18, :]
     for group in range(ROWS):
         tile = kernel_tile(feats_ref[0, group % 2, group // 2], rows1, rows1_sq)
         same = jnp.where(idxt_ref[:, group : group + 1] == row1, ridge_term, 0.0)
         cross_ref[group * GROUP : (group + 1) * GROUP, :] = (tile.astype(F32) + same).astype(BF16)
-
-    def sum_pieces(rcv, lead):
-        total = rcv[0, lead : lead + 16, :].astype(F32)
-        for piece in range(1, PTS):
-            total = total + rcv[piece, lead : lead + 16, :].astype(F32)
-        return total
-
-    def share_rows(at, value):
-        ax_ref[at, me_r] = value.astype(BF16)
-        to_rows(ax_ref.at[at], AX + at)
-
-    def whole_rows(at):
-        wait_bytes(ax_ref.at[at, pl.ds(0, ROWS - 1)], recv_sem.at[AX + at])
-        parts = []
-        for group in range(ROWS):
-            parts += unstack(ax_ref[at, group].astype(F32))
-        return jnp.concatenate(parts, axis=1)
-
-    wait_bytes(rs0_rcv.at[pl.ds(0, PTS - 1)], recv_sem.at[RS0])
-    share_rows(0, sum_pieces(rs0_rcv, 0))
-    wait_bytes(rs1_rcv.at[pl.ds(0, PTS - 1)], recv_sem.at[RS1])
-    share_rows(1, sum_pieces(rs1_rcv, 16))
-    partial1 = sum_pieces(rs1_rcv, 0)
-    make_factor(1)
     loads[3].wait()
 
     def step_of(update, resid):
@@ -354,83 +371,78 @@
 
     def send_steps(update, step):
         chunk_at = jnp.floor(iota((8, 128), 1) * (1.0 / SLOTS))
-        for half in range(2):
-            found = []
-            for part in range(4):
-                group = half * 4 + part
-                found.append(
-                    dot(step[:, group * GROUP : (group + 1) * GROUP], sel_ref[update * ROWS + group])
+        for pair in range(4):
+            cut = slice(pair * 256, pair * 256 + 256)
+            found = [
+                dot(
+                    step[:, group * GROUP : (group + 1) * GROUP],
+                    sel_ref[update * ROWS + group, :, cut],
                 )
-            for owner in range(PTS):
-                block = owner // 4
-                kind = owner % 4
-                total = jnp.zeros((8, 128), F32)
-                for part in range(4):
-                    piece = found[part][:, block * 128 : (block + 1) * 128]
-                    total = jnp.where(chunk_at == float((kind + part) % 4), piece, total)
-                d_snd[update, owner, half] = total
-        for owner in range(PTS):
-            d_out = jnp.concatenate([d_snd[update, owner, 0], d_snd[update, owner, 1]], axis=0)
-            d_rcv[2 + update, owner] = d_out.astype(BF16)
-        to_pts(lambda peer: d_rcv.at[2 + update, peer], d_rcv.at[update], DS + update)
-        d_rcv[update, me_p] = d_rcv[2 + update, me_p]
-
-    resid0 = whole_rows(0)
-    step0 = step_of(0, resid0)
-    base_rows = whole_rows(1)
-    drop = alpha_mix * step_size * momentum_gain + (1.0 - alpha_mix) * step_size
-    moved = (base_rows - drop * step0.astype(F32)).astype(BF16).astype(F32) - base_rows
-    high = moved.astype(BF16)
-    low = (moved - high.astype(F32)).astype(BF16)
-    lhs = jnp.concatenate([high.astype(F32), low.astype(F32)], axis=0).astype(BF16)
-    change = dot(lhs, cross_ref[...])
-    share_rows(2, partial1 + stack(change[:8] + change[8:]))
-    send_steps(0, step0)
-    step1 = step_of(1, whole_rows(2))
-    send_steps(1, step1)
-
-    for update in range(2):
-        wait_bytes(d_rcv.at[update, pl.ds(0, PTS - 1)], recv_sem.at[DS + update])
-        steps_ref[update] = d_rcv[update]
-
-    for update in range(2):
-        wait_bytes(g_rcv.at[update, pl.ds(0, PTS - 1)], send_sem.at[G + update])
-        wait_bytes(feats_ref.at[update, core, pl.ds(0, 3)], send_sem.at[FX + update])
-        wait_bytes(feats_ref.at[update, core], send_sem.at[FC + update])
-        wait_bytes(d_rcv.at[update, pl.ds(0, PTS - 1)], send_sem.at[DS + update])
-    wait_bytes(rs0_rcv.at[pl.ds(0, PTS - 1)], send_sem.at[RS0])
-    wait_bytes(rs1_rcv.at[pl.ds(0, PTS - 1)], send_sem.at[RS1])
-    for at in range(3):
-        wait_bytes(ax_ref.at[at, pl.ds(0, ROWS - 1)], send_sem.at[AX + at])
-
-
-def apply_kernel(w_ref, z_ref, steps_ref, places_ref, w_out, z_out):
-    rows = w_ref.shape[0]
-    first = (pl.program_id(0) * rows).astype(F32)
-
-    def change(update):
+                for group in range(ROWS)
+            ]
+            for at in range(8):
+                owner = pair * 8 + at
+                halves = []
+                for half in range(2):
+                    total = jnp.zeros((8, 128), F32)
+                    for part in range(4):
+                        lanes = slice(at // 4 * 128, at // 4 * 128 + 128)
+                        piece = found[half * 4 + part][:, lanes]
+                        total = jnp.where(chunk_at == float((owner + part) % 4), piece, total)
+                    halves.append(total)
+                d_snd[update, owner] = jnp.concatenate(halves, axis=0).astype(BF16)
+        to_pts(lambda peer: d_snd.at[update, peer], d_rcv.at[update], DS + update)
+        d_rcv[update, me_p] = d_snd[update, me_p]
+
+    def received(update):
+        arrive(DS + update)
         halves = []
         for half in range(2):
             cut = slice(half * 8, half * 8 + 8)
             halves.append(
                 jnp.concatenate(
-                    [steps_ref[update, piece].astype(F32)[cut] for piece in range(PTS)], axis=0
+                    [d_rcv[update, piece].astype(F32)[cut] for piece in range(PTS)], axis=0
                 )
             )
-        steps = jnp.concatenate(halves, axis=1).astype(BF16)
-        place = places_ref[update : update + 1, :]
-        hot = jnp.where(iota((rows, GROUP), 0) + first == place, 1.0, 0.0).astype(BF16)
-        return dot(hot, steps, NT)
-
-    current = w_ref[...]
-    momentum_now = z_ref[...]
-    for update in range(2):
-        delta = change(update)
-        mixed = alpha_mix * momentum_now + (1.0 - alpha_mix) * current
-        current = mixed - step_size * delta
-        momentum_now = (
-            beta_keep * momentum_now + (1.0 - beta_keep) * mixed
-        ) - step_size * momentum_gain * delta
+        return jnp.concatenate(halves, axis=1).astype(BF16)
+
+    step0 = step_of(0, whole_rows(0))
+    drop = alpha_mix * step_size * momentum_gain + (1.0 - alpha_mix) * step_size
+    change = dot(step0, cross_ref[...]) * drop
+    arrive(RS1)
+    share_rows(1, sum_pieces(rs1_rcv) - stack(change))
+    send_steps(0, step0)
+    make_factor(1)
+    step1 = step_of(1, whole_rows(1))
+    send_steps(1, step1)
+
+    steps0 = received(0)
+    for part in range(4):
+        cut = slice(part * 256, part * 256 + 256)
+        current, momentum_now = apply_update(
+            w_ref[cut, :], z_ref[cut, :], steps0, places_ref[0:1, :], part * 256.0
+        )
+        w_ref[cut, :] = current
+        z_ref[cut, :] = momentum_now
+    stores = [
+        pltpu.make_async_copy(src, dst, load_sem.at[at])
+        for at, (src, dst) in enumerate([(w_ref, w_mid), (z_ref, z_mid)])
+    ]
+    for store in stores:
+        store.start()
+    steps_ref[...] = received(1)
+
+    for store in stores:
+        store.wait()
+    for sem, ref in sent:
+        wait_bytes(ref, send_sem.at[sem])
+
+
+def apply_kernel(w_ref, z_ref, steps_ref, places_ref, w_out, z_out):
+    first = (pl.program_id(0) * w_ref.shape[0]).astype(F32)
+    current, momentum_now = apply_update(
+        w_ref[...], z_ref[...], steps_ref[...], places_ref[1:2, :], first
+    )
     w_out[...] = current
     z_out[...] = momentum_now
 
@@ -438,14 +450,16 @@
 def shards(features, targets, coefficients, momentum, block_index, pivot_index, nystrom_core):
     vmem = pl.BlockSpec(memory_space=pltpu.VMEM)
     anywhere = pl.BlockSpec(memory_space=pl.ANY)
-    steps, places = pl.pallas_call(
+    w_mid, z_mid, steps, places = pl.pallas_call(
         block_kernel,
         out_shape=(
-            jax.ShapeDtypeStruct((2, PTS, 16, 128), BF16),
+            jax.ShapeDtypeStruct(coefficients.shape, F32),
+            jax.ShapeDtypeStruct(momentum.shape, F32),
+            jax.ShapeDtypeStruct((256, GROUP), BF16),
             jax.ShapeDtypeStruct((8, GROUP), F32),
         ),
         in_specs=[vmem, vmem, vmem, anywhere, anywhere, anywhere, anywhere],
-        out_specs=(vmem, vmem),
+        out_specs=(anywhere, anywhere, vmem, vmem),
         scratch_shapes=[
             pltpu.VMEM((128, GROUP), F32),
             pltpu.VMEM((GROUP, 128), F32),
@@ -455,24 +469,23 @@
             pltpu.VMEM((2, 512, 512), BF16),
             pltpu.SemaphoreType.DMA((4,)),
             pltpu.VMEM((16, GROUP, PTS * SLOTS), BF16),
-            pltpu.VMEM((2, SLOTS, 128), BF16),
-            pltpu.VMEM((2, PTS, SLOTS, 128), BF16),
+            pltpu.VMEM((2, CAP, 128), BF16),
+            pltpu.VMEM((2, PTS, CAP, 128), BF16),
             pltpu.VMEM((2, 2, 4, GROUP, 128), BF16),
             pltpu.VMEM((2, ROWS * GROUP, 512), BF16),
             pltpu.VMEM((ROWS * GROUP, GROUP), BF16),
             pltpu.VMEM((LOCAL, 256), BF16),
             pltpu.VMEM((LOCAL, 256), BF16),
             pltpu.VMEM((2, GROUP, 256), F32),
-            pltpu.VMEM((GROUP, 256), F32),
             pltpu.VMEM((PTS, 16, 128), BF16),
             pltpu.VMEM((PTS, 16, 128), BF16),
-            pltpu.VMEM((PTS, 32, 128), BF16),
-            pltpu.VMEM((PTS, 32, 128), BF16),
-            pltpu.VMEM((3, ROWS, 16, 128), BF16),
-            pltpu.VMEM((2, PTS, 2, 8, 128), F32),
-            pltpu.VMEM((4, PTS, 16, 128), BF16),
-            pltpu.SemaphoreType.DMA((13,)),
-            pltpu.SemaphoreType.DMA((13,)),
+            pltpu.VMEM((PTS, 16, 128), BF16),
+            pltpu.VMEM((PTS, 16, 128), BF16),
+            pltpu.VMEM((2, ROWS, 16, 128), BF16),
+            pltpu.VMEM((2, PTS, 16, 128), BF16),
+            pltpu.VMEM((2, PTS, 16, 128), BF16),
+            pltpu.SemaphoreType.DMA((12,)),
+            pltpu.SemaphoreType.DMA((12,)),
         ],
         compiler_params=pltpu.CompilerParams(
             collective_id=0, has_side_effects=True, vmem_limit_bytes=56 * 1024 * 1024
@@ -492,12 +505,12 @@
         in_specs=[
             by_rows,
             by_rows,
-            pl.BlockSpec((2, PTS, 16, 128), lambda at: (0, 0, 0, 0)),
+            pl.BlockSpec((256, GROUP), lambda at: (0, 0)),
             pl.BlockSpec((8, GROUP), lambda at: (0, 0)),
         ],
         out_specs=(by_rows, by_rows),
         name="apply_steps",
-    )(coefficients, momentum, steps, places)
+    )(w_mid, z_mid, steps, places)
 
 
 def solution(mesh):

time: 60.4 us -> 52.5 us (0.87)
  Pallas kernels: 59.6 us -> 51.7 us
    pallas_call x1, Pallas kernels: 55.1 us -> 47.5 us  [shards(): pl.pallas_call(block_kernel, out_shape=(jax.ShapeDtypeStruct(coefficients...]
where the time goes in v2:
time: 52.5 us; the launch traced here: 52.4 us
  Pallas kernels  51.7 us (98%)
  between operations  0.64 us (1%)
    pallas_call x1, Pallas kernels, shards(): pl.pallas_call(block_kernel, out_shape=(jax.ShapeDtypeStruct(coefficients...  47.5 us
    pallas_call x1, Pallas kernels, shards(): pl.pallas_call(apply_kernel, grid=(LOCAL // tile,), out_shape=(jax.ShapeD...  4.2 us

profile of v2, /device:TPU:1, one launch (start us, length us, event | category | flops | bytes accessed | tf_op | source)
XLA Modules:
  0.0 52.4 jit_solution(10723292039784573853)
XLA Ops:
  0.6 47.5 %block_steps.1 = (f32[1024,256]{1,0:T(8,128)}, f32[1024,256]{1,0:T(8,128)}, bf16[256,256]{1,0:T(8,128)(2,1)}, f32[8,256]{1,0:T(8,128)}) custom-call(s32[2,2048]{1,0:T(2,128)} %bi_ref.1, s32[2,512]{1,0:T(2,128)} %pv_ref.1, bf16[1024,128]{1,0:T(8,128)(2,1)} %x_ref.1, f32[1024,256]{1,0:T(8,128)} %w_hbm.1, f32[1024,256]{1,0:T(8,128)} %z_hbm.1, ...), custom_call_target="tpu_custom_call" | custom-call | tf_op jit(solution)/shard_map/block_steps/pallas_call | solution.py:453
  48.2 4.2 %apply_steps.1 = (f32[1024,256]{1,0:T(8,128)}, f32[1024,256]{1,0:T(8,128)}) custom-call(f32[1024,256]{1,0:T(8,128)} %get-tuple-element.6.w_ref, f32[1024,256]{1,0:T(8,128)} %get-tuple-element.7.z_ref, bf16[256,256]{1,0:T(8,128)(2,1)} %get-tuple-element.8.steps_ref, f32[8,256]{1,0:T(8,128)} %get-tuple-element.9.places_ref), custom_call_target="tpu_custom_call" | custom-call | tf_op jit(solution)/shard_map/apply_steps/pallas_call | solution.py:498

commit v3 on v2

--- a/solution.py
+++ b/solution.py
@@ -24,6 +24,8 @@
 LOCAL = 1024
 GROUP = 256
 CAP = 24
+VMEM_BYTES = 64_500_000
+STORES = 2
 SLOTS = 32
 
 
@@ -81,7 +83,7 @@
     bi_ref, pv_ref, x_ref, w_hbm, z_hbm, t_hbm, core_hbm,
     w_mid, z_mid, steps_ref, places_ref,
     idx_ref, idxt_ref, w_ref, z_ref, t_ref, core_ref, load_sem,
-    sel_ref, g_snd, g_rcv, feats_ref, factor_ref, cross_ref, mixb_ref, baseb_ref,
+    sel_ref, own_sel_ref, pivot_sel_ref, g_snd, g_rcv, feats_ref, factor_ref, cross_ref, mixb_ref, baseb_ref,
     off_ref, rs0_snd, rs0_rcv, rs1_snd, rs1_rcv, ax_ref, d_snd, d_rcv,
     send_sem, recv_sem,
 ):
@@ -264,13 +266,22 @@
             places_ref[update : update + 1, half * 128 : (half + 1) * 128] = point
 
     slots_iota = iota((GROUP, PTS * CAP), 1)
+    for update in range(2):
+        col = owner_of(idxt_ref[:, 16 + update : 17 + update])
+        slot = rank_col(16 + update)[:, 0:1] + col * CAP
+        own_sel_ref[update] = jnp.where(slots_iota == slot, 1.0, 0.0).astype(BF16)
+        for half in range(2):
+            at = 18 + update * 2 + half
+            col = idxt_ref[:, at : at + 1]
+            for group in range(ROWS):
+                hit = iota((GROUP, GROUP), 1) + float(group * GROUP) == col
+                pivot_sel_ref[update, half, :, group * GROUP : (group + 1) * GROUP] = jnp.where(
+                    hit, 1.0, 0.0
+                ).astype(BF16)
 
     def own_features(update):
         arrive(G + update)
-        col = owner_of(idxt_ref[:, 16 + update : 17 + update])
-        slot = rank_col(16 + update)[:, 0:1] + col * CAP
-        hot = jnp.where(slots_iota == slot, 1.0, 0.0).astype(BF16)
-        rows = dot(hot, g_rcv[update].reshape(PTS * CAP, 128)).astype(BF16)
+        rows = dot(own_sel_ref[update], g_rcv[update].reshape(PTS * CAP, 128)).astype(BF16)
         feats_ref[update, core, chip] = rows
         for hop in range(1, 4):
             pltpu.make_async_remote_copy(
@@ -317,12 +328,10 @@
         arrive(FC + update)
         pivots = []
         for half in range(2):
-            at = 18 + update * 2 + half
-            col = idxt_ref[:, at : at + 1]
             total = jnp.zeros((GROUP, 128), F32)
             for group in range(ROWS):
-                hot = jnp.where(iota((GROUP, GROUP), 1) + float(group * GROUP) == col, 1.0, 0.0)
-                total = total + dot(hot.astype(BF16), feats_ref[update, group % 2, group // 2])
+                hot = pivot_sel_ref[update, half, :, group * GROUP : (group + 1) * GROUP]
+                total = total + dot(hot, feats_ref[update, group % 2, group // 2])
             pivots.append(total.astype(BF16))
         pivots = jnp.concatenate(pivots, axis=0)
         pivots_sq = row_norms(pivots)[0:1]
@@ -351,17 +360,26 @@
             parts += unstack(ax_ref[at, group].astype(F32))
         return jnp.concatenate(parts, axis=1)
 
+    rows1_sq = row_norms(rows1)[0:1]
+    row1 = idx_ref[17:18, :]
+
+    def cross_part(kind):
+        for at in range(4):
+            tile = kernel_tile(feats_ref[0, kind, at], rows1, rows1_sq)
+            col = jnp.where(
+                kind == 0, idxt_ref[:, 2 * at : 2 * at + 1], idxt_ref[:, 2 * at + 1 : 2 * at + 2]
+            )
+            same = jnp.where(col == row1, ridge_term, 0.0)
+            rows = pl.ds(pl.multiple_of((2 * at + kind) * GROUP, GROUP), GROUP)
+            cross_ref[rows, :] = (tile.astype(F32) + same).astype(BF16)
+
     share_with_core(0)
+    cross_part(core)
     arrive(RS0)
     share_rows(0, sum_pieces(rs0_rcv))
     make_factor(0)
     share_with_core(1)
-    rows1_sq = row_norms(rows1)[0:1]
-    row1 = idx_ref[17:18, :]
-    for group in range(ROWS):
-        tile = kernel_tile(feats_ref[0, group % 2, group // 2], rows1, rows1_sq)
-        same = jnp.where(idxt_ref[:, group : group + 1] == row1, ridge_term, 0.0)
-        cross_ref[group * GROUP : (group + 1) * GROUP, :] = (tile.astype(F32) + same).astype(BF16)
+    cross_part(1 - core)
     loads[3].wait()
 
     def step_of(update, resid):
@@ -438,18 +456,46 @@
         wait_bytes(ref, send_sem.at[sem])
 
 
-def apply_kernel(w_ref, z_ref, steps_ref, places_ref, w_out, z_out):
-    first = (pl.program_id(0) * w_ref.shape[0]).astype(F32)
-    current, momentum_now = apply_update(
-        w_ref[...], z_ref[...], steps_ref[...], places_ref[1:2, :], first
-    )
-    w_out[...] = current
-    z_out[...] = momentum_now
+def apply_kernel(
+    w_ref, z_ref, steps_hbm, places_hbm, w_out, z_out,
+    w_now, z_now, steps_ref, places_ref, small_sem, load_sem, store_sem,
+):
+    tile = w_now.shape[0] // STORES
+    loads = []
+    stores = []
+    small = [
+        pltpu.make_async_copy(steps_hbm, steps_ref, small_sem.at[0]),
+        pltpu.make_async_copy(places_hbm, places_ref, small_sem.at[1]),
+    ]
+    for load in small:
+        load.start()
+    for part in range(STORES):
+        cut = pl.ds(part * tile, tile)
+        for at, (src, dst) in enumerate([(w_ref, w_now), (z_ref, z_now)]):
+            loads.append(pltpu.make_async_copy(src.at[cut], dst.at[cut], load_sem.at[at, part]))
+            loads[-1].start()
+    for load in small:
+        load.wait()
+    for part in range(STORES):
+        cut = pl.ds(part * tile, tile)
+        loads[2 * part].wait()
+        loads[2 * part + 1].wait()
+        current, momentum_now = apply_update(
+            w_now[cut, :], z_now[cut, :], steps_ref[...], places_ref[1:2, :], float(part * tile)
+        )
+        w_now[cut, :] = current
+        z_now[cut, :] = momentum_now
+        for at, (src, dst) in enumerate([(w_now, w_out), (z_now, z_out)]):
+            stores.append(pltpu.make_async_copy(src.at[cut], dst.at[cut], store_sem.at[at, part]))
+            stores[-1].start()
+    for store in stores:
+        store.wait()
 
 
 def shards(features, targets, coefficients, momentum, block_index, pivot_index, nystrom_core):
     vmem = pl.BlockSpec(memory_space=pltpu.VMEM)
     anywhere = pl.BlockSpec(memory_space=pl.ANY)
+    hbm = pl.BlockSpec(memory_space=pltpu.HBM)
     w_mid, z_mid, steps, places = pl.pallas_call(
         block_kernel,
         out_shape=(
@@ -458,7 +504,7 @@
             jax.ShapeDtypeStruct((256, GROUP), BF16),
             jax.ShapeDtypeStruct((8, GROUP), F32),
         ),
-        in_specs=[vmem, vmem, vmem, anywhere, anywhere, anywhere, anywhere],
+        in_specs=[vmem, vmem, vmem, hbm, hbm, hbm, hbm],
         out_specs=(anywhere, anywhere, vmem, vmem),
         scratch_shapes=[
             pltpu.VMEM((128, GROUP), F32),
@@ -469,6 +515,8 @@
             pltpu.VMEM((2, 512, 512), BF16),
             pltpu.SemaphoreType.DMA((4,)),
             pltpu.VMEM((16, GROUP, PTS * SLOTS), BF16),
+            pltpu.VMEM((2, GROUP, PTS * CAP), BF16),
+            pltpu.VMEM((2, 2, GROUP, ROWS * GROUP), BF16),
             pltpu.VMEM((2, CAP, 128), BF16),
             pltpu.VMEM((2, PTS, CAP, 128), BF16),
             pltpu.VMEM((2, 2, 4, GROUP, 128), BF16),
@@ -488,27 +536,29 @@
             pltpu.SemaphoreType.DMA((12,)),
         ],
         compiler_params=pltpu.CompilerParams(
-            collective_id=0, has_side_effects=True, vmem_limit_bytes=56 * 1024 * 1024
+            collective_id=0, has_side_effects=True, vmem_limit_bytes=VMEM_BYTES
         ),
         name="block_steps",
     )(block_index, pivot_index, features, coefficients, momentum, targets, nystrom_core)
 
-    tile = 256
-    by_rows = pl.BlockSpec((tile, 256), lambda at: (at, 0))
     return pl.pallas_call(
         apply_kernel,
-        grid=(LOCAL // tile,),
         out_shape=(
             jax.ShapeDtypeStruct(coefficients.shape, F32),
             jax.ShapeDtypeStruct(momentum.shape, F32),
         ),
-        in_specs=[
-            by_rows,
-            by_rows,
-            pl.BlockSpec((256, GROUP), lambda at: (0, 0)),
-            pl.BlockSpec((8, GROUP), lambda at: (0, 0)),
+        in_specs=[hbm, hbm, hbm, hbm],
+        out_specs=(hbm, hbm),
+        scratch_shapes=[
+            pltpu.VMEM((LOCAL, 256), F32),
+            pltpu.VMEM((LOCAL, 256), F32),
+            pltpu.VMEM((256, GROUP), BF16),
+            pltpu.VMEM((8, GROUP), F32),
+            pltpu.SemaphoreType.DMA((2,)),
+            pltpu.SemaphoreType.DMA((2, STORES)),
+            pltpu.SemaphoreType.DMA((2, STORES)),
         ],
-        out_specs=(by_rows, by_rows),
+        compiler_params=pltpu.CompilerParams(vmem_limit_bytes=VMEM_BYTES),
         name="apply_steps",
     )(w_mid, z_mid, steps, places)
 

time: 52.5 us -> 50.8 us (0.968)
  Pallas kernels: 51.7 us -> 49.9 us
    pallas_call x1, Pallas kernels: 4.2 us -> 2.98 us  [shards(): pl.pallas_call(apply_kernel, out_shape=(jax.ShapeDtypeStruct(coefficients...]
    pallas_call x1, Pallas kernels: 47.5 us -> 46.9 us  [shards(): pl.pallas_call(block_kernel, out_shape=(jax.ShapeDtypeStruct(coefficients...]
where the time goes in v3:
time: 50.8 us; the launch traced here: 50.7 us
  Pallas kernels  49.9 us (98%)
  between operations  0.8 us (2%)
    pallas_call x1, Pallas kernels, shards(): pl.pallas_call(block_kernel, out_shape=(jax.ShapeDtypeStruct(coefficients...  46.9 us
    pallas_call x1, Pallas kernels, shards(): pl.pallas_call(apply_kernel, out_shape=(jax.ShapeDtypeStruct(coefficients...  2.98 us

profile of v3, /device:TPU:1, one launch (start us, length us, event | category | flops | bytes accessed | tf_op | source)
XLA Modules:
  0.0 50.7 jit_solution(1291363952567484291)
XLA Ops:
  0.6 46.9 %block_steps.1 = (f32[1024,256]{1,0:T(8,128)}, f32[1024,256]{1,0:T(8,128)}, bf16[256,256]{1,0:T(8,128)(2,1)}, f32[8,256]{1,0:T(8,128)}) custom-call(s32[2,2048]{1,0:T(2,128)} %bi_ref.1, s32[2,512]{1,0:T(2,128)} %pv_ref.1, bf16[1024,128]{1,0:T(8,128)(2,1)} %x_ref.1, f32[1024,256]{1,0:T(8,128)} %w_hbm.1, f32[1024,256]{1,0:T(8,128)} %z_hbm.1, ...), custom_call_target="tpu_custom_call" | custom-call | tf_op jit(solution)/shard_map/block_steps/pallas_call | solution.py:499
  47.5 3.0 %apply_steps.1 = (f32[1024,256]{1,0:T(8,128)}, f32[1024,256]{1,0:T(8,128)}) custom-call(f32[1024,256]{1,0:T(8,128)} %get-tuple-element.6.w_ref, f32[1024,256]{1,0:T(8,128)} %get-tuple-element.7.z_ref, bf16[256,256]{1,0:T(8,128)(2,1)} %get-tuple-element.8.steps_hbm, f32[8,256]{1,0:T(8,128)} %get-tuple-element.9.places_hbm), custom_call_target="tpu_custom_call" | custom-call | tf_op jit(solution)/shard_map/apply_steps/pallas_call | solution.py:544

commit v4 on v3

--- a/solution.py
+++ b/solution.py
@@ -178,17 +178,22 @@
 
     pl.semaphore_wait(barrier, PTS + ROWS - 2)
 
+    deep = PTS // 4
+    peer_y = [lax.rem(me_p // deep + step, 4) * deep for step in range(4)]
+    peer_z = [lax.rem(me_p + step, deep) for step in range(deep)]
+    farthest_first = sorted(
+        ((step, hop) for step in range(4) for hop in range(deep) if step or hop),
+        key=lambda at: -min(at[0], 4 - at[0]) - min(at[1], deep - at[1]),
+    )
+
     def to_pts(src_of, dst, sem):
-        def send(hop, carry):
-            peer = lax.rem(me_p + hop, PTS)
+        for step, hop in farthest_first:
+            peer = peer_y[step] + peer_z[hop]
             pltpu.make_async_remote_copy(
                 src_ref=src_of(peer), dst_ref=dst.at[me_p],
                 send_sem=send_sem.at[sem], recv_sem=recv_sem.at[sem],
                 device_id={"pts": peer}, device_id_type=MESH,
             ).start()
-            return carry
-
-        lax.fori_loop(1, PTS, send, 0)
         expect(sem, dst.at[pl.ds(0, PTS - 1)])
 
     def to_rows(buf, sem):
@@ -409,7 +414,7 @@
                         total = jnp.where(chunk_at == float((owner + part) % 4), piece, total)
                     halves.append(total)
                 d_snd[update, owner] = jnp.concatenate(halves, axis=0).astype(BF16)
-        to_pts(lambda peer: d_snd.at[update, peer], d_rcv.at[update], DS + update)
+        to_pts(lambda peer: d_snd.at[update].at[peer], d_rcv.at[update], DS + update)
         d_rcv[update, me_p] = d_snd[update, me_p]
 
     def received(update):

time: 50.8 us -> 51.1 us (level)
  no operation moved by 1% of the time
where the time goes in v4:
time: 51.1 us; the launch traced here: 51 us
  Pallas kernels  50.2 us (98%)
  between operations  0.8 us (2%)
    pallas_call x1, Pallas kernels, shards(): pl.pallas_call(block_kernel, out_shape=(jax.ShapeDtypeStruct(coefficients...  47.2 us
    pallas_call x1, Pallas kernels, shards(): pl.pallas_call(apply_kernel, out_shape=(jax.ShapeDtypeStruct(coefficients...  2.98 us

profile of v4, /device:TPU:1, one launch (start us, length us, event | category | flops | bytes accessed | tf_op | source)
XLA Modules:
  0.0 51.0 jit_solution(5617698836435992105)
XLA Ops:
  0.6 47.2 %block_steps.1 = (f32[1024,256]{1,0:T(8,128)}, f32[1024,256]{1,0:T(8,128)}, bf16[256,256]{1,0:T(8,128)(2,1)}, f32[8,256]{1,0:T(8,128)}) custom-call(s32[2,2048]{1,0:T(2,128)} %bi_ref.1, s32[2,512]{1,0:T(2,128)} %pv_ref.1, bf16[1024,128]{1,0:T(8,128)(2,1)} %x_ref.1, f32[1024,256]{1,0:T(8,128)} %w_hbm.1, f32[1024,256]{1,0:T(8,128)} %z_hbm.1, ...), custom_call_target="tpu_custom_call" | custom-call | tf_op jit(solution)/shard_map/block_steps/pallas_call | solution.py:504
  47.8 3.0 %apply_steps.1 = (f32[1024,256]{1,0:T(8,128)}, f32[1024,256]{1,0:T(8,128)}) custom-call(f32[1024,256]{1,0:T(8,128)} %get-tuple-element.6.w_ref, f32[1024,256]{1,0:T(8,128)} %get-tuple-element.7.z_ref, bf16[256,256]{1,0:T(8,128)(2,1)} %get-tuple-element.8.steps_hbm, f32[8,256]{1,0:T(8,128)} %get-tuple-element.9.places_hbm), custom_call_target="tpu_custom_call" | custom-call | tf_op jit(solution)/shard_map/apply_steps/pallas_call | solution.py:549

commit v5 on v4

--- a/solution.py
+++ b/solution.py
@@ -80,9 +80,9 @@
 
 
 def block_kernel(
-    bi_ref, pv_ref, x_ref, w_hbm, z_hbm, t_hbm, core_hbm,
+    bi_hbm, pv_hbm, x_hbm, w_hbm, z_hbm, t_hbm, core_hbm,
     w_mid, z_mid, steps_ref, places_ref,
-    idx_ref, idxt_ref, w_ref, z_ref, t_ref, core_ref, load_sem,
+    bi_ref, pv_ref, x_ref, idx_ref, idxt_ref, w_ref, z_ref, t_ref, core_ref, load_sem,
     sel_ref, own_sel_ref, pivot_sel_ref, g_snd, g_rcv, feats_ref, factor_ref, cross_ref, mixb_ref, baseb_ref,
     off_ref, rs0_snd, rs0_rcv, rs1_snd, rs1_rcv, ax_ref, d_snd, d_rcv,
     send_sem, recv_sem,
@@ -96,11 +96,20 @@
 
     barrier = pltpu.get_barrier_semaphore()
 
-    def greet_pts(hop, carry):
-        pl.semaphore_signal(
-            barrier, inc=1, device_id={"pts": lax.rem(me_p + hop, PTS)}, device_id_type=MESH
-        )
-        return carry
+    first_loads = [
+        pltpu.make_async_copy(src, dst, load_sem.at[4 + at])
+        for at, (src, dst) in enumerate([(bi_hbm, bi_ref), (pv_hbm, pv_ref), (x_hbm, x_ref)])
+    ]
+    for load in first_loads:
+        load.start()
+
+    deep = PTS // 4
+    peer_y = [lax.rem(me_p // deep + step, 4) * deep for step in range(4)]
+    peer_z = [lax.rem(me_p + step, deep) for step in range(deep)]
+    farthest_first = sorted(
+        ((step, hop) for step in range(4) for hop in range(deep) if step or hop),
+        key=lambda at: -min(at[0], 4 - at[0]) - min(at[1], deep - at[1]),
+    )
 
     def greet_rows(hop, carry):
         pl.semaphore_signal(
@@ -108,7 +117,10 @@
         )
         return carry
 
-    lax.fori_loop(1, PTS, greet_pts, 0)
+    for step, hop in farthest_first:
+        pl.semaphore_signal(
+            barrier, inc=1, device_id={"pts": peer_y[step] + peer_z[hop]}, device_id_type=MESH
+        )
     lax.fori_loop(1, ROWS, greet_rows, 0)
 
     loads = [
@@ -134,6 +146,8 @@
         wait_bytes(arrivals.pop(sem), recv_sem.at[sem])
 
     idx_ref[...] = jnp.zeros_like(idx_ref)
+    for load in first_loads:
+        load.wait()
     for update in range(2):
         for group in range(ROWS):
             at = update * ROWS + group
@@ -177,14 +191,6 @@
         g_snd[update] = dot(place, x_ref[...]).astype(BF16)
 
     pl.semaphore_wait(barrier, PTS + ROWS - 2)
-
-    deep = PTS // 4
-    peer_y = [lax.rem(me_p // deep + step, 4) * deep for step in range(4)]
-    peer_z = [lax.rem(me_p + step, deep) for step in range(deep)]
-    farthest_first = sorted(
-        ((step, hop) for step in range(4) for hop in range(deep) if step or hop),
-        key=lambda at: -min(at[0], 4 - at[0]) - min(at[1], deep - at[1]),
-    )
 
     def to_pts(src_of, dst, sem):
         for step, hop in farthest_first:
@@ -509,16 +515,19 @@
             jax.ShapeDtypeStruct((256, GROUP), BF16),
             jax.ShapeDtypeStruct((8, GROUP), F32),
         ),
-        in_specs=[vmem, vmem, vmem, hbm, hbm, hbm, hbm],
+        in_specs=[hbm] * 7,
         out_specs=(anywhere, anywhere, vmem, vmem),
         scratch_shapes=[
+            pltpu.VMEM(block_index.shape, jnp.int32),
+            pltpu.VMEM(pivot_index.shape, jnp.int32),
+            pltpu.VMEM(features.shape, BF16),
             pltpu.VMEM((128, GROUP), F32),
             pltpu.VMEM((GROUP, 128), F32),
             pltpu.VMEM((LOCAL, 256), F32),
             pltpu.VMEM((LOCAL, 256), F32),
             pltpu.VMEM((LOCAL, 256), BF16),
             pltpu.VMEM((2, 512, 512), BF16),
-            pltpu.SemaphoreType.DMA((4,)),
+            pltpu.SemaphoreType.DMA((7,)),
             pltpu.VMEM((16, GROUP, PTS * SLOTS), BF16),
             pltpu.VMEM((2, GROUP, PTS * CAP), BF16),
             pltpu.VMEM((2, 2, GROUP, ROWS * GROUP), BF16),

time: 51.1 us -> 50.3 us (0.984)
  Pallas kernels: 50.2 us -> 49.4 us
    pallas_call x1, Pallas kernels: 47.2 us -> 46.4 us  [shards(): pl.pallas_call(block_kernel, out_shape=(jax.ShapeDtypeStruct(coefficients...]
where the time goes in v5:
time: 50.3 us; the launch traced here: 50.2 us
  Pallas kernels  49.4 us (98%)
  between operations  0.8 us (2%)
    pallas_call x1, Pallas kernels, shards(): pl.pallas_call(block_kernel, out_shape=(jax.ShapeDtypeStruct(coefficients...  46.4 us
    pallas_call x1, Pallas kernels, shards(): pl.pallas_call(apply_kernel, out_shape=(jax.ShapeDtypeStruct(coefficients...  2.98 us

profile of v5, /device:TPU:1, one launch (start us, length us, event | category | flops | bytes accessed | tf_op | source)
XLA Modules:
  0.0 50.2 jit_solution(2449799755924404832)
XLA Ops:
  0.6 46.4 %block_steps.1 = (f32[1024,256]{1,0:T(8,128)}, f32[1024,256]{1,0:T(8,128)}, bf16[256,256]{1,0:T(8,128)(2,1)}, f32[8,256]{1,0:T(8,128)}) custom-call(s32[2,2048]{1,0:T(2,128)} %bi_hbm.1, s32[2,512]{1,0:T(2,128)} %pv_hbm.1, bf16[1024,128]{1,0:T(8,128)(2,1)} %x_hbm.1, f32[1024,256]{1,0:T(8,128)} %w_hbm.1, f32[1024,256]{1,0:T(8,128)} %z_hbm.1, ...), custom_call_target="tpu_custom_call" | custom-call | tf_op jit(solution)/shard_map/block_steps/pallas_call | solution.py:510
  47.0 3.0 %apply_steps.1 = (f32[1024,256]{1,0:T(8,128)}, f32[1024,256]{1,0:T(8,128)}) custom-call(f32[1024,256]{1,0:T(8,128)} %get-tuple-element.6.w_ref, f32[1024,256]{1,0:T(8,128)} %get-tuple-element.7.z_ref, bf16[256,256]{1,0:T(8,128)(2,1)} %get-tuple-element.8.steps_hbm, f32[8,256]{1,0:T(8,128)} %get-tuple-element.9.places_hbm), custom_call_target="tpu_custom_call" | custom-call | tf_op jit(solution)/shard_map/apply_steps/pallas_call | solution.py:558
